TPU v7x, 32 devices: a whole 2x2x4 slice. The times are simulated.
32 devices in a mesh: tok: 8 (over y, x, core), mdl: 4 (over z).
Axes of the slice: x: 2, y: 2, z: 4, core: 2. Of those that a mesh axis runs over, the one named last changes fastest.
Arguments:
- hidden_states: bfloat16 [4096, 3072], P('tok', 'mdl'), may hold values from -36 to 36
- lengths: int32 [2], replicated, may hold values from 1 to 2277, 3644 in all
- positions: int32 [3, 4096], P(None, 'tok'), may hold values from 0 to 44, as said below
- modulation: float32 [6, 3072], replicated, may hold values from -3 to 3
- query_weight: bfloat16 [3072, 3072], P('tok', 'mdl'), may hold values from -1.1 to 1.1
- key_weight: bfloat16 [3072, 3072], P('tok', 'mdl'), may hold values from -1.1 to 1.1
- value_weight: bfloat16 [3072, 3072], P('tok', 'mdl'), may hold values from -0.109375 to 0.109375
- out_weight: bfloat16 [3072, 3072], P('tok', 'mdl'), may hold values from -0.109375 to 0.109375
- query_gain: float32 [64], replicated, may hold values from 0.1 to 1.9
- key_gain: float32 [64], replicated, may hold values from 0.1 to 1.9
Outputs:
- updated: bfloat16 [4096, 3072], P('tok', 'mdl')
Inputs may be any that keep to these rules, and one draw needn't show every extreme that they name: lengths[0] + lengths[1] = 3644, and neither of them exceeds 2277. `positions`: frame below 13, row below 30, column below 45.
All inputs are finite; a program needn't handle non-finite values.
Results may differ from a plain program's by a relative error of at most 0.0045.
Values may be sent and summed in bfloat16 or wider, within the bound.
A program may use at most 128 MiB of HBM per device.

v0:
```python
import functools
import jax
import jax.numpy as jnp
from jax import lax
from jax.experimental import pallas as pl
from jax.experimental.pallas import tpu as pltpu
from jax.sharding import PartitionSpec as P

TEXT = 226


def token_labels(row_index, lengths):
    bound = TEXT + lengths[0]
    request = (row_index >= bound).astype(jnp.int32)
    place = row_index - request * bound
    return (request, place < TEXT, bound)


def modulate(rows_bf, modulation, is_text):
    values = rows_bf.astype(jnp.float32)
    center = values - jnp.mean(values, axis=1, keepdims=True)
    spread = jnp.mean(center * center, axis=1, keepdims=True)
    normal = center * lax.rsqrt(spread + 1e-05)
    textual = is_text[:, None]
    shift = jnp.where(textual, modulation[3][None, :], modulation[0][None, :])
    scale = jnp.where(textual, modulation[4][None, :], modulation[1][None, :])
    return (normal * (1.0 + scale) + shift).astype(jnp.bfloat16)


def pair_angles(positions, pairs):
    index = jnp.arange(pairs, dtype=jnp.int32)
    first = pairs // 4
    second = (pairs - first) // 2
    third = pairs - first - second
    component = jnp.where(index < first, 0, jnp.where(index < first + second, 1, 2))
    local = index - jnp.where(component == 0, 0, jnp.where(component == 1, first, first + second))
    count = jnp.where(component == 0, first, jnp.where(component == 1, second, third))
    rates = jnp.power(jnp.float32(10000.0), -local.astype(jnp.float32) / count.astype(jnp.float32))
    places = positions.astype(jnp.float32)
    chosen = jnp.where(
        component[:, None] == 0,
        places[0][None, :],
        jnp.where(component[:, None] == 1, places[1][None, :], places[2][None, :]),
    )
    return jnp.transpose(chosen * rates[:, None])


def head_norm(projected, gain, angles, is_text):
    width = gain.shape[0]
    shaped = projected.reshape(projected.shape[0], -1, width)
    center = shaped - jnp.mean(shaped, axis=2, keepdims=True)
    spread = jnp.mean(center * center, axis=2, keepdims=True)
    normal = center * lax.rsqrt(spread + 1e-06) * gain
    half = width // 2
    cosine = jnp.cos(angles)[:, None, :]
    sine = jnp.sin(angles)[:, None, :]
    lower = normal[:, :, :half]
    upper = normal[:, :, half:]
    turned = jnp.concatenate([lower * cosine - upper * sine, lower * sine + upper * cosine], axis=2)
    return jnp.where(is_text[:, None, None], normal, turned).astype(jnp.bfloat16)


def gather_kernel(n_tok, n_mdl, n_row, n_col, *refs):
    rows_in = refs[:n_row]
    cols_in = refs[n_row : n_row + n_col]
    outs = refs[n_row + n_col : 2 * (n_row + n_col)]
    rows_out, cols_out = outs[:n_row], outs[n_row:]
    (
        local_sem,
        send1,
        recv1,
        send2,
        recv2,
        send3,
        recv3,
        to_right,
        from_left,
        to_left,
        from_right,
    ) = refs[2 * (n_row + n_col) :]
    square = n_tok == 8
    chips = n_tok // 2
    tok, mdl = lax.axis_index("tok"), lax.axis_index("mdl")
    chip, core = tok // 2, tok % 2
    sibling = chip * 2 + 1 - core

    def chip_at(step):
        if square:
            return (chip, chip + 1 - 2 * (chip % 2), (chip + 2) % 4, 3 - chip)[step]
        return (chip + step) % chips

    def source_at(step):
        return chip_at(step) if square else chip_at(chips - step)

    barrier = pltpu.get_barrier_semaphore()
    greeted = 0
    if n_row:
        for step in (1, 2) if square else range(1, chips):
            pl.semaphore_signal(
                barrier, inc=1, device_id={"tok": chip_at(step) * 2 + core, "mdl": mdl}
            )
            greeted += 1
        pl.semaphore_signal(barrier, inc=1, device_id={"tok": sibling, "mdl": mdl})
        greeted += 1
    if n_col:
        for side in (1, n_mdl - 1):
            pl.semaphore_signal(
                barrier, inc=1, device_id={"tok": tok, "mdl": (mdl + side) % n_mdl}
            )
            greeted += 1
    pl.semaphore_wait(barrier, greeted)

    def row_block(number, owner):
        size = rows_in[number].shape[0]
        return rows_out[number].at[pl.ds(pl.multiple_of(owner * size, size), size), :]

    def col_block(number, owner):
        size = cols_in[number].shape[1]
        return cols_out[number].at[:, pl.ds(pl.multiple_of(owner * size, size), size)]

    def direct(number, step):
        target = chip_at(step) * 2 + core if step else sibling
        return pltpu.make_async_remote_copy(
            src_ref=rows_in[number],
            dst_ref=row_block(number, tok),
            send_sem=send1.at[number, step],
            recv_sem=recv1.at[number, step],
            device_id={"tok": target, "mdl": mdl},
        )

    def passed(number, step):
        block = row_block(number, source_at(step) * 2 + core)
        return pltpu.make_async_remote_copy(
            src_ref=block,
            dst_ref=block,
            send_sem=send2.at[number, step],
            recv_sem=recv2.at[number, step],
            device_id={"tok": sibling, "mdl": mdl},
        )

    def relayed(number, step):
        half = rows_in[number].shape[0] // 2
        first = (source_at(step) * 2 + core) * 2 * half + (step - 1) * half
        block = rows_out[number].at[pl.ds(pl.multiple_of(first, half), half), :]
        return pltpu.make_async_remote_copy(
            src_ref=block,
            dst_ref=block,
            send_sem=send3.at[number, step],
            recv_sem=recv3.at[number, step],
            device_id={"tok": chip_at(3 - step) * 2 + core, "mdl": mdl},
        )

    directs = (1, 2) if square else range(1, chips)

    def rightward(number, step):
        block = col_block(number, mdl - step)
        return pltpu.make_async_remote_copy(
            src_ref=block if step else cols_in[number],
            dst_ref=block,
            send_sem=to_right.at[number, step],
            recv_sem=from_left.at[number, step],
            device_id={"tok": tok, "mdl": mdl + 1},
        )

    def leftward(number, step):
        block = col_block(number, mdl + step)
        return pltpu.make_async_remote_copy(
            src_ref=block if step else cols_in[number],
            dst_ref=block,
            send_sem=to_left.at[number, step],
            recv_sem=from_right.at[number, step],
            device_id={"tok": tok, "mdl": mdl - 1},
        )

    def right_if(step):
        return (mdl >= step) & (mdl < n_mdl - 1)

    def left_if(step):
        return (mdl + step < n_mdl) & (mdl > 0)

    for number in range(n_col):
        @pl.when(right_if(0))
        def _():
            rightward(number, 0).start()

        @pl.when(left_if(0))
        def _():
            leftward(number, 0).start()

    for number in range(n_row):
        for step in directs:
            direct(number, step).start()
        direct(number, 0).start()
    locals_ = []
    for number in range(n_row):
        locals_.append(
            pltpu.make_async_copy(rows_in[number], row_block(number, tok), local_sem.at[number])
        )
    for number in range(n_col):
        locals_.append(
            pltpu.make_async_copy(
                cols_in[number], col_block(number, mdl), local_sem.at[n_row + number]
            )
        )
    for copy in locals_:
        copy.start()

    def finish_diagonal(number):
        for step in (1, 2):
            relayed(number, step).wait_recv()
        passed(number, 3).start()

    for turn in range(max(n_row, n_mdl - 1 if n_col else 0)):
        hop = turn + 1
        if hop < n_mdl:
            for number in range(n_col):
                @pl.when(mdl >= hop)
                def _():
                    rightward(number, hop - 1).wait_recv()

                @pl.when(right_if(hop))
                def _():
                    rightward(number, hop).start()

                @pl.when(mdl + hop < n_mdl)
                def _():
                    leftward(number, hop - 1).wait_recv()

                @pl.when(left_if(hop))
                def _():
                    leftward(number, hop).start()

        if turn < n_row:
            for step in directs:
                direct(turn, step).wait_recv()
                if square:
                    relayed(turn, step).start()
                passed(turn, step).start()
            if square and turn > 0:
                finish_diagonal(turn - 1)

    if square and n_row:
        finish_diagonal(n_row - 1)
    for copy in locals_:
        copy.wait()
    for number in range(n_row):
        direct(number, 0).wait()
        for step in directs:
            direct(number, step).wait_send()
            if square:
                relayed(number, step).wait_send()
        for step in range(1, chips):
            passed(number, step).wait()
    for number in range(n_col):
        for step in range(n_mdl - 1):
            @pl.when(right_if(step))
            def _():
                rightward(number, step).wait_send()

            @pl.when(left_if(step))
            def _():
                leftward(number, step).wait_send()


def gather_all(mesh, over_tok, over_mdl, collective_id):
    n_tok, n_mdl = mesh.shape["tok"], mesh.shape["mdl"]
    n_row, n_col = len(over_tok), len(over_mdl)
    shapes = [
        jax.ShapeDtypeStruct((one.shape[0] * n_tok, one.shape[1]), one.dtype) for one in over_tok
    ] + [jax.ShapeDtypeStruct((one.shape[0], one.shape[1] * n_mdl), one.dtype) for one in over_mdl]
    chips = n_tok // 2
    row_sem = pltpu.SemaphoreType.DMA((max(n_row, 1), chips))
    col_sem = pltpu.SemaphoreType.DMA((max(n_col, 1), n_mdl))
    return pl.pallas_call(
        functools.partial(gather_kernel, n_tok, n_mdl, n_row, n_col),
        out_shape=shapes,
        in_specs=[pl.BlockSpec(memory_space=pl.ANY)] * (n_row + n_col),
        out_specs=[pl.BlockSpec(memory_space=pl.ANY)] * (n_row + n_col),
        scratch_shapes=[pltpu.SemaphoreType.DMA((n_row + n_col,))] + [row_sem] * 6 + [col_sem] * 4,
        compiler_params=pltpu.CompilerParams(collective_id=collective_id, has_side_effects=True),
        name=f"gather_{collective_id}",
    )(*over_tok, *over_mdl)


def attend_kernel(rows_at_once, keys_at_once, head_width, meta_ref, q_ref, k_ref, v_ref, o_ref):
    bound, first_row = meta_ref[0], meta_ref[1]
    own_rows, lanes = q_ref.shape
    count = k_ref.shape[0]
    chunks = count // keys_at_once
    per = lanes // head_width
    lane = lax.broadcasted_iota(jnp.int32, (1, lanes), 1) // head_width
    masks = [(lane == head).astype(jnp.float32) for head in range(per)]
    edge = bound // keys_at_once
    edge_start = pl.multiple_of(edge * keys_at_once, keys_at_once)
    edge_keys = edge_start + lax.broadcasted_iota(jnp.int32, (keys_at_once, 1), 0)

    for block in range(own_rows // rows_at_once):
        rows = pl.ds(block * rows_at_once, rows_at_once)
        start = first_row + block * rows_at_once
        row_ids = start + lax.broadcasted_iota(jnp.int32, (rows_at_once, 1), 0)

        def add_chunk(carry, keys, values):
            queries = q_ref[rows, :]
            result = []
            for head in range(per):
                mine = queries * (masks[head] * head_width ** (-0.5)).astype(jnp.bfloat16)
                score = lax.dot_general(
                    mine, keys, (((1,), (1,)), ((), ())), preferred_element_type=jnp.float32
                )
                expo = jnp.exp(score).astype(jnp.bfloat16)
                result.append(
                    carry[head]
                    + jnp.dot(expo, values[head], preferred_element_type=jnp.float32)
                )
            return tuple(result)

        def inner(chunk, carry):
            here = pl.ds(pl.multiple_of(chunk * keys_at_once, keys_at_once), keys_at_once)
            values = v_ref[here, :]
            with_ones = [
                values * mask.astype(jnp.bfloat16) + (1.0 - mask).astype(jnp.bfloat16)
                for mask in masks
            ]
            return add_chunk(carry, k_ref[here, :], with_ones)

        for request in range(2):
            active = start < bound if request == 0 else start + rows_at_once > bound

            @pl.when(active)
            def _():
                here = pl.ds(edge_start, keys_at_once)
                inside = edge_keys < bound if request == 0 else edge_keys >= bound
                wide = v_ref[here, :].astype(jnp.float32)
                with_ones = [
                    jnp.where(inside, wide * mask + (1.0 - mask), 0.0).astype(jnp.bfloat16)
                    for mask in masks
                ]
                zero = jnp.zeros((rows_at_once, lanes), jnp.float32)
                carry = add_chunk((zero,) * per, k_ref[here, :], with_ones)
                if request == 0:
                    low, high = 0, edge
                else:
                    low, high = edge + 1, chunks
                carry = lax.fori_loop(low, high, inner, carry)
                output = zero
                for head in range(per):
                    total = pltpu.roll(carry[head], head_width, axis=1)
                    output = jnp.where(lane == head, carry[head] / total, output)
                if request == 0:
                    o_ref[rows, :] = output.astype(o_ref.dtype)
                else:
                    old = o_ref[rows, :].astype(jnp.float32)
                    o_ref[rows, :] = jnp.where(row_ids >= bound, output, old).astype(o_ref.dtype)


def attend(query, keys, values, bound, first_row, head_width, part, parts):
    width = query.shape[1]
    own_rows = query.shape[0] // parts
    count = keys.shape[0]
    lanes = 2 * head_width
    meta = jnp.stack([bound, first_row + part * own_rows]).astype(jnp.int32)
    block = pl.BlockSpec((own_rows, lanes), lambda pair, meta: (part, pair))
    out_block = pl.BlockSpec((own_rows, lanes), lambda pair, meta: (0, pair))
    full = pl.BlockSpec((count, lanes), lambda pair, meta: (0, pair))
    return pl.pallas_call(
        functools.partial(attend_kernel, 256, 512, head_width),
        out_shape=jax.ShapeDtypeStruct((own_rows, width), jnp.bfloat16),
        grid_spec=pltpu.PrefetchScalarGridSpec(
            num_scalar_prefetch=1,
            grid=(width // lanes,),
            in_specs=[block, full, full],
            out_specs=out_block,
        ),
        compiler_params=pltpu.CompilerParams(vmem_limit_bytes=58 * 2**20),
        cost_estimate=pl.CostEstimate(
            flops=4 * own_rows * count * width,
            bytes_accessed=4 * count * width,
            transcendentals=own_rows * count * width // head_width,
        ),
        name=f"attend_{part}",
    )(meta, query, keys, values)


def shards(
    mesh,
    hidden_states,
    lengths,
    positions,
    modulation,
    query_weight,
    key_weight,
    value_weight,
    out_weight,
    query_gain,
    key_gain,
):
    own_rows = hidden_states.shape[0]
    local_width = query_weight.shape[1]
    head_width = query_gain.shape[0]
    local_heads = local_width // head_width
    key_full, value_full, query_full, full_rows = gather_all(
        mesh, [key_weight, value_weight, query_weight], [hidden_states], 0
    )
    row_index = lax.axis_index("tok") * own_rows + jnp.arange(own_rows, dtype=jnp.int32)
    request, is_text, bound = token_labels(row_index, lengths)
    normed = modulate(full_rows, modulation, is_text)
    angles = pair_angles(positions, head_width // 2)
    pieces = (query_full, key_full, value_full)
    columns = normed
    query_sum, key_sum, value_sum = tuple(
        (
            jnp.dot(columns, pieces[number], preferred_element_type=jnp.float32)
            for number in range(3)
        )
    )
    query = head_norm(query_sum, query_gain, angles, is_text)
    key_flat = head_norm(key_sum, key_gain, angles, is_text).reshape(own_rows, local_width)
    value_flat = value_sum.astype(jnp.bfloat16)
    keys, values = gather_all(mesh, [key_flat, value_flat], [], 1)
    query_flat = query.reshape(own_rows, local_width)
    first_row = lax.axis_index("tok") * own_rows
    first, second = (
        attend(query_flat, keys, values, bound, first_row, head_width, part, 2)
        for part in range(2)
    )
    first_heads = lax.all_gather(first, "mdl", axis=1, tiled=True)
    out_full, second_heads = gather_all(mesh, [out_weight], [second], 2)
    out_width = out_weight.shape[1]
    projected = jnp.concatenate(
        [
            jnp.dot(heads, out_full, preferred_element_type=jnp.float32)
            for heads in (first_heads, second_heads)
        ],
        axis=0,
    )
    gate_rows = lax.dynamic_slice_in_dim(
        modulation, lax.axis_index("mdl") * out_width, out_width, 1
    )
    gate = jnp.where(is_text[:, None], gate_rows[5][None, :], gate_rows[2][None, :])
    return (hidden_states.astype(jnp.float32) + gate * projected).astype(jnp.bfloat16)


def solution(mesh):
    return jax.shard_map(
        functools.partial(shards, mesh),
        mesh=mesh,
        in_specs=(
            P("tok", "mdl"),
            P(),
            P(None, "tok"),
            P(),
            P("tok", "mdl"),
            P("tok", "mdl"),
            P("tok", "mdl"),
            P("tok", "mdl"),
            P(),
            P(),
        ),
        out_specs=P("tok", "mdl"),
        check_vma=False,
    )
```

profile of v0, /device:TPU:0, one launch (start us, length us, event | category | flops | bytes accessed | tf_op | source)
XLA Modules:
  0.0 300.1 jit_solution(13157613594888128731)
XLA Ops:
  6.5 0.0 all-gather.2.cloned.1.call-start
  6.6 84.5 %gather_0.1 = (bf16[3072,768]{1,0:T(8,128)(2,1)}, bf16[3072,768]{1,0:T(8,128)(2,1)}, bf16[3072,768]{1,0:T(8,128)(2,1)}, bf16[512,3072]{1,0:T(8,128)(2,1)}) custom-call(bf16[384,768]{1,0:T(8,128)(2,1)} %refs_0_.2, bf16[384,768]{1,0:T(8,128)(2,1)} %refs_1_.1, bf16[384,768]{1,0:T(8,128)(2,1)} %refs_2_.1, bf16[512,768]{1,0:T(8,128)(2,1)} %refs_3_.1), custom_call_target="tpu_custom_call" | custom-call | tf_op jit(solution)/shard_map/gather_0/pallas_call | solution.py:274
  91.1 0.0 copy-start
  91.1 2.5 convert_reduce_fusion
  93.7 0.3 copy-done
  94.0 1.0 fusion.2
  94.9 0.0 copy-done.11
  95.0 0.0 copy-done.16
  95.0 0.0 copy-start.15
  95.1 2.8 fusion.5
  97.8 0.0 copy-start.7
  97.9 1.6 copy-done.7
  99.5 0.0 copy-done.15
  99.5 2.6 fusion.14
  102.1 0.0 copy-start.1
  102.1 0.5 copy.11
  102.5 0.7 copy-done.1
  103.2 0.2 reduce_sum.56
  103.5 0.3 multiply_reduce_fusion.1
  103.7 7.1 %fusion.15 = f32[512,768]{1,0:T(8,128)} fusion(bf16[512,3072]{1,0:T(8,128)(2,1)} %copy-done.7, bf16[3072,768]{1,0:T(8,128)(2,1)} %get-tuple-element.15), kind=kOutput, calls=%fused_computation.49 | convolution fusion | flops 2415919104 | bytes 9437184 | tf_op jit(solution)/shard_map/dot_general | solution.py:412
  110.8 1.9 copy.15
  112.7 0.0 copy-start.12
  112.7 0.0 copy-start.13
  112.7 0.0 copy-start.14
  112.7 0.2 reduce_sum.58
  112.9 0.2 multiply_reduce_fusion
  113.2 0.2 copy-done.12
  113.4 0.0 copy-done.13
  113.4 0.0 copy-done.14
  113.4 0.6 multiply_multiply_fusion
  114.0 0.3 fusion.9
  114.4 0.5 multiply_subtract_fusion
  114.9 0.1 pad_maximum_fusion
  115.0 1.2 copy.14
  116.3 0.1 pad_maximum_fusion.1
  116.3 1.2 copy.18
  117.5 0.2 mul.170
  117.7 0.5 copy.13
  118.1 0.2 mul.189
  118.3 1.7 copy.17
  120.0 0.2 sub.61
  120.2 1.6 copy.12
  121.8 0.2 sub.67
  122.0 1.6 copy.16
  123.6 0.1 mul.174
  123.7 0.1 mul.193
  123.8 0.0 copy-start.9
  123.8 0.0 copy-start.10
  123.8 6.9 %convolution_convert_fusion.refs_1_ = bf16[512,768]{1,0:T(8,128)(2,1)} fusion(bf16[512,3072]{1,0:T(8,128)(2,1)} %copy-done.7, bf16[3072,768]{1,0:T(8,128)(2,1)} %get-tuple-element.16), kind=kOutput, calls=%fused_computation.19 | convolution fusion | flops 2416312320 | bytes 8650752 | tf_op jit(solution)/shard_map/dot_general | solution.py:412
  130.7 0.6 pad_add_fusion.meta_ref
  131.3 0.0 copy-done.2
  131.4 2.1 select_convert_fusion
  133.5 56.9 %gather_1.1 = (bf16[4096,768]{1,0:T(8,128)(2,1)}, bf16[4096,768]{1,0:T(8,128)(2,1)}) custom-call(bf16[512,768]{1,0:T(8,128)(2,1)} %get-tuple-element.38.refs_0_, bf16[512,768]{1,0:T(8,128)(2,1)} %convolution_convert_fusion.refs_1_), custom_call_target="tpu_custom_call" | custom-call | tf_op jit(solution)/shard_map/gather_1/pallas_call | solution.py:274
  190.4 22.3 %attend_0.1 = bf16[256,768]{1,0:T(8,128)(2,1)} custom-call(s32[2]{0:T(128)} %pad_add_fusion.meta_ref, bf16[512,768]{1,0:T(8,128)(2,1)} %get-tuple-element.39.q_ref, bf16[4096,768]{1,0:T(8,128)(2,1)} %get-tuple-element.17.k_ref, bf16[4096,768]{1,0:T(8,128)(2,1)} %get-tuple-element.18.v_ref), custom_call_target="tpu_custom_call" | custom-call | flops 3221225472 | bytes 12582912 | tf_op jit(solution)/shard_map/attend_0/pallas_call | solution.py:365
  212.6 0.0 all-gather.2.cloned.1.call-update
  212.7 0.6 pad_add_fusion.1.meta_ref
  213.2 22.3 %attend_1.1.refs_1_ = bf16[256,768]{1,0:T(8,128)(2,1)} custom-call(s32[2]{0:T(128)} %pad_add_fusion.1.meta_ref, bf16[512,768]{1,0:T(8,128)(2,1)} %get-tuple-element.39.q_ref, bf16[4096,768]{1,0:T(8,128)(2,1)} %get-tuple-element.17.k_ref, bf16[4096,768]{1,0:T(8,128)(2,1)} %get-tuple-element.18.v_ref), custom_call_target="tpu_custom_call" | custom-call | flops 3221225472 | bytes 12582912 | tf_op jit(solution)/shard_map/attend_1/pallas_call | solution.py:365
  235.5 47.9 %gather_2.1 = (bf16[3072,768]{1,0:T(8,128)(2,1)}, bf16[256,3072]{1,0:T(8,128)(2,1)}) custom-call(bf16[384,768]{1,0:T(8,128)(2,1)} %refs_0_.3, bf16[256,768]{1,0:T(8,128)(2,1)} %attend_1.1.refs_1_), custom_call_target="tpu_custom_call" | custom-call | tf_op jit(solution)/shard_map/gather_2/pallas_call | solution.py:274
  283.4 0.1 dynamic-slice_reduce_fusion.1
  283.5 4.2 %fusion.17 = f32[256,768]{1,0:T(8,128)S(1)} fusion(bf16[256,3072]{1,0:T(8,128)(2,1)} %get-tuple-element.20, bf16[3072,768]{1,0:T(8,128)(2,1)} %get-tuple-element.19), kind=kOutput, calls=%fused_computation.51 | convolution fusion | flops 1207959552 | bytes 7077888 | tf_op jit(solution)/shard_map/dot_general | solution.py:431
  287.7 0.0 copy-start.8
  287.7 0.0 all-gather.2.cloned.1.call-done
  287.7 4.3 %fusion.16 = f32[256,768]{1,0:T(8,128)S(1)} fusion(bf16[256,3072]{1,0:T(8,128)(2,1)} %all-gather.2.cloned.1.call-done, bf16[3072,768]{1,0:T(8,128)(2,1)} %get-tuple-element.19), kind=kOutput, calls=%fused_computation.50 | convolution fusion | flops 1207959552 | bytes 7077888 | tf_op jit(solution)/shard_map/dot_general | solution.py:431
  292.0 1.2 fusion.7
  (28 shorter events, 0.2 us)
Async XLA Ops:
  6.5 281.2 %all-gather.2.cloned.1.call-start = ((), (), s32[]{:S(2)}) async-start(), calls=%async_computation | async-start | bytes 1966080 | tf_op jit(solution)/shard_map/all_gather | solution.py:426
  91.1 2.8 copy-start
  94.0 1.0 copy-start.11
  94.0 1.0 copy-start.16
  95.0 4.4 %copy-start.15 = (bf16[3072,768]{1,0:T(8,128)(2,1)S(1)}, bf16[3072,768]{1,0:T(8,128)(2,1)}, u32[]{:S(2)}) copy-start(bf16[3072,768]{1,0:T(8,128)(2,1)} %get-tuple-element.14) | copy-start | bytes 14155780
  97.8 1.6 copy-start.7
  102.1 1.2 copy-start.1
  112.7 0.7 copy-start.12
  112.7 0.7 copy-start.13
  112.7 0.7 copy-start.14
  123.8 7.5 %copy-start.2 = (f32[512,768]{1,0:T(8,128)S(1)}, f32[512,768]{1,0:T(8,128)}, u32[]{:S(2)}) copy-start(f32[512,768]{1,0:T(8,128)} %copy-done.1) | copy-start | bytes 4718596
  123.8 7.5 %copy-start.3 = (f32[512,768]{1,0:T(8,128)S(1)}, f32[512,768]{1,0:T(8,128)}, u32[]{:S(2)}) copy-start(f32[512,768]{1,0:T(8,128)} %fusion.15) | copy-start | bytes 4718596
  123.8 7.5 %copy-start.4 = (f32[512,768]{1,0:T(8,128)S(1)}, f32[512,768]{1,0:T(8,128)}, u32[]{:S(2)}) copy-start(f32[512,768]{1,0:T(8,128)} %copy.17) | copy-start | bytes 4718596
  123.8 7.5 %copy-start.5 = (f32[512,768]{1,0:T(8,128)S(1)}, f32[512,768]{1,0:T(8,128)}, u32[]{:S(2)}) copy-start(f32[512,768]{1,0:T(8,128)} %copy.12) | copy-start | bytes 4718596
  123.8 7.5 %copy-start.6 = (f32[512,768]{1,0:T(8,128)S(1)}, f32[512,768]{1,0:T(8,128)}, u32[]{:S(2)}) copy-start(f32[512,768]{1,0:T(8,128)} %copy.16) | copy-start | bytes 4718596
  123.8 7.5 %copy-start.9 = (bf16[512,768]{1,0:T(8,128)(2,1)S(1)}, bf16[512,768]{1,0:T(8,128)(2,1)}, u32[]{:S(2)}) copy-start(bf16[512,768]{1,0:T(8,128)(2,1)} %copy.14) | copy-start | bytes 2359300
  123.8 7.5 %copy-start.10 = (bf16[512,768]{1,0:T(8,128)(2,1)S(1)}, bf16[512,768]{1,0:T(8,128)(2,1)}, u32[]{:S(2)}) copy-start(bf16[512,768]{1,0:T(8,128)(2,1)} %copy.18) | copy-start | bytes 2359300
  287.7 4.3 %copy-start.8 = (bf16[512,768]{1,0:T(8,128)(2,1)S(1)}, bf16[512,768]{1,0:T(8,128)(2,1)}, u32[]{:S(2)}) copy-start(bf16[512,768]{1,0:T(8,128)(2,1)} %refs_3_.1) | copy-start | bytes 2359300
Sparse Core Ops, SparseCore 0:
  212.8 35.5 all-gather.1
where the time goes:
time: 300 us
  Pallas kernels  234 us (78%)
  matrix products  25 us (8%)
  local copies, waits for them, and re-layouts  14 us (5%)
  between operations  13.8 us (5%)
  other arithmetic  13.4 us (4%)
    pallas_call x3, Pallas kernels, gather_all(): pl.pallas_call(functools.partial(gather_kernel, n_tok, n_mdl, n_row, n_co...  189 us
    pallas_call x2, Pallas kernels, attend(): pl.pallas_call(functools.partial(attend_kernel, 256, 512, head_width), ou...  44.5 us
    dot_general x3, matrix products, shards(): jnp.dot(columns, pieces[number], preferred_element_type=jnp.float32)  16.6 us
    dot_general x2, matrix products, shards(): jnp.dot(heads, out_full, preferred_element_type=jnp.float32)  8.45 us
  transfers between devices with their start and end apart: 1, of which 0 were waited for; matrix products, arithmetic and copies ran while one was open for 2% of the time, Pallas kernels for 23%

commit v1 on v0

--- a/solution.py
+++ b/solution.py
@@ -45,26 +45,18 @@
     return jnp.transpose(chosen * rates[:, None])
 
 
-def head_norm(projected, gain, angles, is_text):
-    width = gain.shape[0]
-    shaped = projected.reshape(projected.shape[0], -1, width)
-    center = shaped - jnp.mean(shaped, axis=2, keepdims=True)
-    spread = jnp.mean(center * center, axis=2, keepdims=True)
-    normal = center * lax.rsqrt(spread + 1e-06) * gain
-    half = width // 2
-    cosine = jnp.cos(angles)[:, None, :]
-    sine = jnp.sin(angles)[:, None, :]
-    lower = normal[:, :, :half]
-    upper = normal[:, :, half:]
-    turned = jnp.concatenate([lower * cosine - upper * sine, lower * sine + upper * cosine], axis=2)
-    return jnp.where(is_text[:, None, None], normal, turned).astype(jnp.bfloat16)
-
-
 def gather_kernel(n_tok, n_mdl, n_row, n_col, *refs):
-    rows_in = refs[:n_row]
-    cols_in = refs[n_row : n_row + n_col]
-    outs = refs[n_row + n_col : 2 * (n_row + n_col)]
-    rows_out, cols_out = outs[:n_row], outs[n_row:]
+    count = n_row + n_col
+    ins, outs = refs[:count], refs[count : 2 * count]
+    exchange(
+        n_tok, n_mdl, ins[:n_row], ins[n_row:], outs[:n_row], outs[n_row:], refs[2 * count :]
+    )
+
+
+def exchange(
+    n_tok, n_mdl, rows_in, cols_in, rows_out, cols_out, semaphores, prepare=None, between=None
+):
+    n_row, n_col = len(rows_in), len(cols_in)
     (
         local_sem,
         send1,
@@ -77,7 +69,7 @@
         from_left,
         to_left,
         from_right,
-    ) = refs[2 * (n_row + n_col) :]
+    ) = semaphores
     square = n_tok == 8
     chips = n_tok // 2
     tok, mdl = lax.axis_index("tok"), lax.axis_index("mdl")
@@ -187,32 +179,33 @@
         def _():
             leftward(number, 0).start()
 
-    for number in range(n_row):
-        for step in directs:
-            direct(number, step).start()
-        direct(number, 0).start()
     locals_ = []
-    for number in range(n_row):
-        locals_.append(
-            pltpu.make_async_copy(rows_in[number], row_block(number, tok), local_sem.at[number])
-        )
     for number in range(n_col):
         locals_.append(
             pltpu.make_async_copy(
                 cols_in[number], col_block(number, mdl), local_sem.at[n_row + number]
             )
         )
-    for copy in locals_:
-        copy.start()
+        locals_[-1].start()
+    for number in range(n_row):
+        if prepare is not None:
+            prepare(number)
+        for step in directs:
+            direct(number, step).start()
+        direct(number, 0).start()
+        locals_.append(
+            pltpu.make_async_copy(rows_in[number], row_block(number, tok), local_sem.at[number])
+        )
+        locals_[-1].start()
 
     def finish_diagonal(number):
         for step in (1, 2):
             relayed(number, step).wait_recv()
         passed(number, 3).start()
 
-    for turn in range(max(n_row, n_mdl - 1 if n_col else 0)):
+    for turn in range(max(n_row, n_mdl - 2 if n_col else 0)):
         hop = turn + 1
-        if hop < n_mdl:
+        if hop < n_mdl - 1:
             for number in range(n_col):
                 @pl.when(mdl >= hop)
                 def _():
@@ -238,11 +231,22 @@
                 passed(turn, step).start()
             if square and turn > 0:
                 finish_diagonal(turn - 1)
+        if between is not None:
+            between(turn)
 
     if square and n_row:
         finish_diagonal(n_row - 1)
     for copy in locals_:
         copy.wait()
+    for number in range(n_col):
+        @pl.when(mdl >= n_mdl - 1)
+        def _():
+            rightward(number, n_mdl - 2).wait_recv()
+
+        @pl.when(mdl + n_mdl - 1 < n_mdl)
+        def _():
+            leftward(number, n_mdl - 2).wait_recv()
+
     for number in range(n_row):
         direct(number, 0).wait()
         for step in directs:
@@ -262,21 +266,130 @@
                 leftward(number, step).wait_send()
 
 
+def exchange_semaphores(n_tok, n_mdl, n_row, n_col):
+    row_sem = pltpu.SemaphoreType.DMA((max(n_row, 1), n_tok // 2))
+    col_sem = pltpu.SemaphoreType.DMA((max(n_col, 1), n_mdl))
+    return [pltpu.SemaphoreType.DMA((n_row + n_col,))] + [row_sem] * 6 + [col_sem] * 4
+
+
+def project_kernel(n_tok, n_mdl, head_width, *refs):
+    normed, key_w, value_w, query_w, key_gain, query_gain, cosine, sine = refs[:8]
+    keys_out, values_out, query_out = refs[8:11]
+    keys, values, query, key_held, value_held, query_held, load_sem = refs[11:18]
+    width = keys.shape[1]
+    lanes = 2 * head_width
+    block = 256 if width % 256 == 0 else lanes
+    loads = [
+        pltpu.make_async_copy(source, held, load_sem.at[number])
+        for number, (source, held) in enumerate(
+            ((key_w, key_held), (value_w, value_held), (query_w, query_held))
+        )
+    ]
+    for load in loads:
+        load.start()
+    lane = lax.broadcasted_iota(jnp.int32, (1, lanes), 1)
+    first = lane < head_width
+    early = lane % head_width < head_width // 2
+
+    def head_mean(terms):
+        one = jnp.sum(jnp.where(first, terms, 0.0), axis=1, keepdims=True)
+        other = jnp.sum(jnp.where(first, 0.0, terms), axis=1, keepdims=True)
+        return jnp.where(first, one, other) * (1.0 / head_width)
+
+    def finished(summed, gain):
+        center = summed - head_mean(summed)
+        normal = center * lax.rsqrt(head_mean(center * center) + 1e-06) * gain[...]
+        partner = jnp.where(
+            early,
+            pltpu.roll(normal, lanes - head_width // 2, axis=1),
+            pltpu.roll(normal, head_width // 2, axis=1),
+        )
+        return normal * cosine[...] + partner * sine[...]
+
+    def project(held, gain, target):
+        def step(number, carry):
+            columns = pl.ds(pl.multiple_of(number * block, block), block)
+            summed = jnp.dot(
+                normed[...], held[:, columns], preferred_element_type=jnp.float32
+            )
+            if gain is not None:
+                summed = jnp.concatenate(
+                    [
+                        finished(summed[:, start : start + lanes], gain)
+                        for start in range(0, block, lanes)
+                    ],
+                    axis=1,
+                )
+            target[:, columns] = summed.astype(jnp.bfloat16)
+            return carry
+
+        lax.fori_loop(0, width // block, step, 0)
+
+    def prepare(number):
+        loads[number].wait()
+        if number == 0:
+            project(key_held, key_gain, keys)
+        else:
+            project(value_held, None, values)
+
+    query_copy = pltpu.make_async_copy(query, query_out, load_sem.at[3])
+
+    def between(turn):
+        if turn == 0:
+            loads[2].wait()
+            project(query_held, query_gain, query)
+            query_copy.start()
+
+    exchange(
+        n_tok,
+        n_mdl,
+        (keys, values),
+        (),
+        (keys_out, values_out),
+        (),
+        refs[18:],
+        prepare,
+        between,
+    )
+    query_copy.wait()
+
+
+def project_and_gather(mesh, normed, weights, gains, cosine, sine, head_width, collective_id):
+    n_tok, n_mdl = mesh.shape["tok"], mesh.shape["mdl"]
+    own_rows, depth = normed.shape
+    width = weights[0].shape[1]
+    full = jax.ShapeDtypeStruct((own_rows * n_tok, width), jnp.bfloat16)
+    own = jax.ShapeDtypeStruct((own_rows, width), jnp.bfloat16)
+    anywhere = pl.BlockSpec(memory_space=pl.ANY)
+    inside = pl.BlockSpec(memory_space=pltpu.VMEM)
+    return pl.pallas_call(
+        functools.partial(project_kernel, n_tok, n_mdl, head_width),
+        out_shape=[full, full, own],
+        in_specs=[inside] + [anywhere] * 3 + [inside] * 4,
+        out_specs=[anywhere] * 3,
+        scratch_shapes=[pltpu.VMEM((own_rows, width), jnp.bfloat16)] * 3
+        + [pltpu.VMEM((depth, width), jnp.bfloat16)] * 3
+        + [pltpu.SemaphoreType.DMA((4,))]
+        + exchange_semaphores(n_tok, n_mdl, 2, 0),
+        compiler_params=pltpu.CompilerParams(
+            collective_id=collective_id, has_side_effects=True, vmem_limit_bytes=48 * 2**20
+        ),
+        name="project_and_gather",
+    )(normed, *weights, *gains, cosine, sine)
+
+
 def gather_all(mesh, over_tok, over_mdl, collective_id):
     n_tok, n_mdl = mesh.shape["tok"], mesh.shape["mdl"]
     n_row, n_col = len(over_tok), len(over_mdl)
     shapes = [
         jax.ShapeDtypeStruct((one.shape[0] * n_tok, one.shape[1]), one.dtype) for one in over_tok
     ] + [jax.ShapeDtypeStruct((one.shape[0], one.shape[1] * n_mdl), one.dtype) for one in over_mdl]
-    chips = n_tok // 2
-    row_sem = pltpu.SemaphoreType.DMA((max(n_row, 1), chips))
-    col_sem = pltpu.SemaphoreType.DMA((max(n_col, 1), n_mdl))
     return pl.pallas_call(
         functools.partial(gather_kernel, n_tok, n_mdl, n_row, n_col),
         out_shape=shapes,
         in_specs=[pl.BlockSpec(memory_space=pl.ANY)] * (n_row + n_col),
         out_specs=[pl.BlockSpec(memory_space=pl.ANY)] * (n_row + n_col),
-        scratch_shapes=[pltpu.SemaphoreType.DMA((n_row + n_col,))] + [row_sem] * 6 + [col_sem] * 4,
+        scratch_shapes=exchange_semaphores(n_tok, n_mdl, n_row, n_col),
         compiler_params=pltpu.CompilerParams(collective_id=collective_id, has_side_effects=True),
         name=f"gather_{collective_id}",
     )(*over_tok, *over_mdl)
@@ -395,9 +508,7 @@
     key_gain,
 ):
     own_rows = hidden_states.shape[0]
-    local_width = query_weight.shape[1]
     head_width = query_gain.shape[0]
-    local_heads = local_width // head_width
     key_full, value_full, query_full, full_rows = gather_all(
         mesh, [key_weight, value_weight, query_weight], [hidden_states], 0
     )
@@ -405,19 +516,20 @@
     request, is_text, bound = token_labels(row_index, lengths)
     normed = modulate(full_rows, modulation, is_text)
     angles = pair_angles(positions, head_width // 2)
-    pieces = (query_full, key_full, value_full)
-    columns = normed
-    query_sum, key_sum, value_sum = tuple(
-        (
-            jnp.dot(columns, pieces[number], preferred_element_type=jnp.float32)
-            for number in range(3)
-        )
-    )
-    query = head_norm(query_sum, query_gain, angles, is_text)
-    key_flat = head_norm(key_sum, key_gain, angles, is_text).reshape(own_rows, local_width)
-    value_flat = value_sum.astype(jnp.bfloat16)
-    keys, values = gather_all(mesh, [key_flat, value_flat], [], 1)
-    query_flat = query.reshape(own_rows, local_width)
+    textual = is_text[:, None]
+    cosine = jnp.tile(jnp.where(textual, 1.0, jnp.cos(angles)), (1, 4))
+    sine = jnp.where(textual, 0.0, jnp.sin(angles))
+    sine = jnp.tile(jnp.concatenate([-sine, sine], axis=1), (1, 2))
+    keys, values, query_flat = project_and_gather(
+        mesh,
+        normed,
+        (key_full, value_full, query_full),
+        [jnp.tile(gain, 2)[None, :] for gain in (key_gain, query_gain)],
+        cosine,
+        sine,
+        head_width,
+        1,
+    )
     first_row = lax.axis_index("tok") * own_rows
     first, second = (
         attend(query_flat, keys, values, bound, first_row, head_width, part, 2)

time: 300 us -> 281 us (0.937); the launches traced: 300 us -> 278 us
  matrix products: 25 us -> 8.45 us
  local copies, waits for them, and re-layouts: 14 us -> 1.77 us
  Pallas kernels: 234 us -> 244 us
  other arithmetic: 13.4 us -> 10.1 us
    pallas_call x0 -> x1, Pallas kernels: none -> 63.9 us  [project_and_gather(): pl.pallas_call(functools.partial(project_kernel, n_tok, n_mdl, head_width...]
    pallas_call x3 -> x2, Pallas kernels: 189 us -> 143 us  [gather_all(): pl.pallas_call(functools.partial(gather_kernel, n_tok, n_mdl, n_row, n_co...]
    dot_general x3 -> x0, matrix products: 16.6 us -> none  [shards(): jnp.dot(columns, pieces[number], preferred_element_type=jnp.float32)]
    pallas_call x2, Pallas kernels: 44.5 us -> 37.5 us  [attend(): pl.pallas_call(functools.partial(attend_kernel, 256, 512, head_width), ou...]
    sub x4 -> x0, local copies, waits for them, and re-layouts: 3.63 us -> none  [head_norm(): center = shaped - jnp.mean(shaped, axis=2, keepdims=True)]
  transfers between devices with their start and end apart: 1 -> 1, of which waited for: 0 -> 0; matrix products, arithmetic and copies ran while one was open for 2% -> 2% of each run, Pallas kernels for 23% -> 28%
where the time goes in v1:
time: 281 us; the launch traced here: 278 us
  Pallas kernels  244 us (87%)
  between operations  13.7 us (5%)
  other arithmetic  10.1 us (4%)
  matrix products  8.45 us (3%)
    pallas_call x2, Pallas kernels, gather_all(): pl.pallas_call(functools.partial(gather_kernel, n_tok, n_mdl, n_row, n_co...  143 us
    pallas_call x1, Pallas kernels, project_and_gather(): pl.pallas_call(functools.partial(project_kernel, n_tok, n_mdl, head_width...  63.9 us
    pallas_call x2, Pallas kernels, attend(): pl.pallas_call(functools.partial(attend_kernel, 256, 512, head_width), ou...  37.5 us
    dot_general x2, matrix products, shards(): jnp.dot(heads, out_full, preferred_element_type=jnp.float32)  8.45 us
  transfers between devices with their start and end apart: 1, of which 0 were waited for; matrix products, arithmetic and copies ran while one was open for 2% of the time, Pallas kernels for 28%

profile of v1, /device:TPU:0, one launch (start us, length us, event | category | flops | bytes accessed | tf_op | source)
XLA Modules:
  0.0 278.0 jit_solution(2075849592350684164)
XLA Ops:
  6.5 0.0 copy-start.3
  6.5 0.0 copy-start.4
  6.5 0.0 copy-start.5
  6.5 0.0 all-gather.2.cloned.1.call-start
  6.6 84.5 %gather_0.1 = (bf16[3072,768]{1,0:T(8,128)(2,1)}, bf16[3072,768]{1,0:T(8,128)(2,1)}, bf16[3072,768]{1,0:T(8,128)(2,1)}, bf16[512,3072]{1,0:T(8,128)(2,1)}) custom-call(bf16[384,768]{1,0:T(8,128)(2,1)} %refs_0_.2, bf16[384,768]{1,0:T(8,128)(2,1)} %refs_1_.1, bf16[384,768]{1,0:T(8,128)(2,1)} %refs_2_.1, bf16[512,768]{1,0:T(8,128)(2,1)} %refs_3_.1), custom_call_target="tpu_custom_call" | custom-call | tf_op jit(solution)/shard_map/gather_0/pallas_call | solution.py:387
  91.1 0.0 copy-start.1
  91.1 0.0 copy-start.6
  91.1 0.0 copy-start.7
  91.2 2.5 convert_reduce_fusion
  93.7 0.3 copy-done.1
  94.0 1.0 fusion.2
  94.9 0.0 copy-done.3
  95.0 0.0 copy-done.4
  95.0 0.0 copy-done.5
  95.1 0.3 fusion.10
  95.5 0.1 copy.12.refs_7_
  95.6 0.1 copy.11.refs_6_
  95.8 0.0 copy-done.6
  95.8 0.1 broadcast_in_dim_tile.6.refs_4_
  95.9 0.0 copy-done.7
  95.9 0.1 broadcast_in_dim_tile.7.refs_5_
  96.0 0.6 pad_add_fusion.meta_ref
  96.6 3.8 %fusion.5.refs_0_ = bf16[512,3072]{1,0:T(8,128)(2,1)S(1)} fusion(bf16[512,3072]{1,0:T(8,128)(2,1)} %get-tuple-element.14, f32[3072]{0:T(1024)S(1)} %bitcast.21, f32[3072]{0:T(1024)S(1)} %bitcast.22, f32[3072]{0:T(1024)S(1)} %bitcast.20, f32[3072]{0:T(1024)S(1)} %bitcast.19, f32[512]{0:T(512)S(1)} %add_rsqrt_fusion, f32[512]{0:T(512)S(1)} %broadcast_multiply_fusion, ...), kind=kLoop, calls=%fused_computation.7 | loop fusion | flops 14155776 | bytes 6345216 | tf_op jit(solution)/shard_map/convert_element_type | solution.py:27
  100.4 63.9 %project_and_gather.1 = (bf16[4096,768]{1,0:T(8,128)(2,1)}, bf16[4096,768]{1,0:T(8,128)(2,1)}, bf16[512,768]{1,0:T(8,128)(2,1)S(1)}) custom-call(bf16[512,3072]{1,0:T(8,128)(2,1)S(1)} %fusion.5.refs_0_, bf16[3072,768]{1,0:T(8,128)(2,1)} %get-tuple-element.15.refs_1_, bf16[3072,768]{1,0:T(8,128)(2,1)} %get-tuple-element.16.refs_2_, ...), custom_call_target="tpu_custom_call" | custom-call | tf_op jit(solution)/shard_map/project_and_gather/pallas_call | solution.py:365
  164.3 0.0 copy-start
  164.3 0.9 copy-done
  165.2 18.7 %attend_0.1 = bf16[256,768]{1,0:T(8,128)(2,1)} custom-call(s32[2]{0:T(128)} %pad_add_fusion.meta_ref, bf16[512,768]{1,0:T(8,128)(2,1)} %copy-done, bf16[4096,768]{1,0:T(8,128)(2,1)} %get-tuple-element.19.k_ref, bf16[4096,768]{1,0:T(8,128)(2,1)} %get-tuple-element.20.v_ref), custom_call_target="tpu_custom_call" | custom-call | flops 3221225472 | bytes 12582912 | tf_op jit(solution)/shard_map/attend_0/pallas_call | solution.py:478
  183.9 0.0 all-gather.2.cloned.1.call-update
  183.9 0.6 pad_add_fusion.1.meta_ref
  184.5 18.8 %attend_1.1.refs_1_ = bf16[256,768]{1,0:T(8,128)(2,1)} custom-call(s32[2]{0:T(128)} %pad_add_fusion.1.meta_ref, bf16[512,768]{1,0:T(8,128)(2,1)} %copy-done, bf16[4096,768]{1,0:T(8,128)(2,1)} %get-tuple-element.19.k_ref, bf16[4096,768]{1,0:T(8,128)(2,1)} %get-tuple-element.20.v_ref), custom_call_target="tpu_custom_call" | custom-call | flops 3221225472 | bytes 12582912 | tf_op jit(solution)/shard_map/attend_1/pallas_call | solution.py:478
  203.3 58.0 %gather_2.1 = (bf16[3072,768]{1,0:T(8,128)(2,1)}, bf16[256,3072]{1,0:T(8,128)(2,1)}) custom-call(bf16[384,768]{1,0:T(8,128)(2,1)} %refs_0_.3, bf16[256,768]{1,0:T(8,128)(2,1)} %attend_1.1.refs_1_), custom_call_target="tpu_custom_call" | custom-call | tf_op jit(solution)/shard_map/gather_2/pallas_call | solution.py:387
  261.3 0.1 dynamic-slice_reduce_fusion.1
  261.4 4.2 %fusion.14 = f32[256,768]{1,0:T(8,128)S(1)} fusion(bf16[256,3072]{1,0:T(8,128)(2,1)} %get-tuple-element.22, bf16[3072,768]{1,0:T(8,128)(2,1)} %get-tuple-element.21), kind=kOutput, calls=%fused_computation.34 | convolution fusion | flops 1207959552 | bytes 7077888 | tf_op jit(solution)/shard_map/dot_general | solution.py:543
  265.6 0.0 copy-start.2
  265.6 0.0 all-gather.2.cloned.1.call-done
  265.7 4.3 %fusion.13 = f32[256,768]{1,0:T(8,128)S(1)} fusion(bf16[256,3072]{1,0:T(8,128)(2,1)} %all-gather.2.cloned.1.call-done, bf16[3072,768]{1,0:T(8,128)(2,1)} %get-tuple-element.21), kind=kOutput, calls=%fused_computation.33 | convolution fusion | flops 1207959552 | bytes 7077888 | tf_op jit(solution)/shard_map/dot_general | solution.py:543
  269.9 0.0 copy-done.2
  269.9 1.2 fusion.7
  (13 shorter events, 0.1 us)
Async XLA Ops:
  6.5 88.4 %copy-start.3 = (f32[6,3072]{1,0:T(8,128)S(1)}, f32[6,3072]{1,0:T(8,128)}, u32[]{:S(2)}) copy-start(f32[6,3072]{1,0:T(8,128)} %param.13) | copy-start | bytes 221188
  6.5 88.4 %copy-start.4 = (s32[3,512]{1,0:T(4,128)S(1)}, s32[3,512]{1,0:T(4,128)}, u32[]{:S(2)}) copy-start(s32[3,512]{1,0:T(4,128)} %param.12) | copy-start | bytes 18436
  6.5 88.5 %copy-start.5 = (s32[2]{0:T(128)S(1)}, s32[2]{0:T(128)}, u32[]{:S(2)}) copy-start(s32[2]{0:T(128)} %param.11) | copy-start | bytes 28
  6.5 259.1 %all-gather.2.cloned.1.call-start = ((), (), s32[]{:S(2)}) async-start(), calls=%async_computation | async-start | bytes 1966080 | tf_op jit(solution)/shard_map/all_gather | solution.py:538
  91.1 2.8 %copy-start.1 = (bf16[512,3072]{1,0:T(8,128)(2,1)S(1)}, bf16[512,3072]{1,0:T(8,128)(2,1)}, u32[]{:S(2)}) copy-start(bf16[512,3072]{1,0:T(8,128)(2,1)} %get-tuple-element.14) | copy-start | bytes 9437188
  91.1 4.6 %copy-start.6 = (f32[64]{0:T(128)S(1)}, f32[64]{0:T(128)}, u32[]{:S(2)}) copy-start(f32[64]{0:T(128)} %param.19) | copy-start | bytes 772
  91.1 4.7 %copy-start.7 = (f32[64]{0:T(128)S(1)}, f32[64]{0:T(128)}, u32[]{:S(2)}) copy-start(f32[64]{0:T(128)} %param.18) | copy-start | bytes 772
  164.3 0.9 copy-start
  265.6 4.3 %copy-start.2 = (bf16[512,768]{1,0:T(8,128)(2,1)S(1)}, bf16[512,768]{1,0:T(8,128)(2,1)}, u32[]{:S(2)}) copy-start(bf16[512,768]{1,0:T(8,128)(2,1)} %refs_3_.1) | copy-start | bytes 2359300
Sparse Core Ops, SparseCore 0:
  184.0 61.0 all-gather.1

commit v2 on v1

--- a/solution.py
+++ b/solution.py
@@ -509,8 +509,9 @@
 ):
     own_rows = hidden_states.shape[0]
     head_width = query_gain.shape[0]
-    key_full, value_full, query_full, full_rows = gather_all(
-        mesh, [key_weight, value_weight, query_weight], [hidden_states], 0
+    full_rows = lax.all_gather(hidden_states, "mdl", axis=1, tiled=True)
+    key_full, value_full, query_full = gather_all(
+        mesh, [key_weight, value_weight, query_weight], [], 0
     )
     row_index = lax.axis_index("tok") * own_rows + jnp.arange(own_rows, dtype=jnp.int32)
     request, is_text, bound = token_labels(row_index, lengths)

time: 281 us -> 257 us (0.915); the launches traced: 278 us -> 258 us
  Pallas kernels: 244 us -> 221 us
    pallas_call x2, Pallas kernels: 143 us -> 113 us  [gather_all(): pl.pallas_call(functools.partial(gather_kernel, n_tok, n_mdl, n_row, n_co...]
    pallas_call x2, Pallas kernels: 37.5 us -> 44.5 us  [attend(): pl.pallas_call(functools.partial(attend_kernel, 256, 512, head_width), ou...]
  transfers between devices with their start and end apart: 1 -> 2, of which waited for: 0 -> 0; matrix products, arithmetic and copies ran while one was open for 2% -> 3% of each run, Pallas kernels for 28% -> 52%
where the time goes in v2:
time: 257 us; the launch traced here: 258 us
  Pallas kernels  221 us (86%)
  between operations  14.2 us (6%)
  other arithmetic  9.81 us (4%)
  matrix products  8.45 us (3%)
  local copies, waits for them, and re-layouts  3.09 us (1%)
    pallas_call x2, Pallas kernels, gather_all(): pl.pallas_call(functools.partial(gather_kernel, n_tok, n_mdl, n_row, n_co...  113 us
    pallas_call x1, Pallas kernels, project_and_gather(): pl.pallas_call(functools.partial(project_kernel, n_tok, n_mdl, head_width...  64.2 us
    pallas_call x2, Pallas kernels, attend(): pl.pallas_call(functools.partial(attend_kernel, 256, 512, head_width), ou...  44.5 us
    dot_general x2, matrix products, shards(): jnp.dot(heads, out_full, preferred_element_type=jnp.float32)  8.45 us
  transfers between devices with their start and end apart: 2, of which 0 were waited for; matrix products, arithmetic and copies ran while one was open for 3% of the time, Pallas kernels for 52%

profile of v2, /device:TPU:0, one launch (start us, length us, event | category | flops | bytes accessed | tf_op | source)
XLA Modules:
  0.0 257.7 jit_solution(12181136377047410376)
XLA Ops:
  6.5 0.0 copy-start.3
  6.5 0.0 all-gather.3.cloned.1.call-start
  6.5 0.7 all-gather.3.cloned.1.call-update
  7.3 0.0 all-gather.5.cloned.1.call-start
  7.3 0.7 convert_element_type.33
  8.7 0.3 fusion.10
  9.1 0.1 copy.12.refs_7_
  9.3 0.1 copy.11.refs_6_
  9.4 0.7 tile.12
  10.1 0.1 broadcast_in_dim_tile.6.refs_4_
  10.1 0.7 tile.13
  10.8 0.1 broadcast_in_dim_tile.7.refs_5_
  10.9 64.9 %gather_0.1 = (bf16[3072,768]{1,0:T(8,128)(2,1)}, bf16[3072,768]{1,0:T(8,128)(2,1)}, bf16[3072,768]{1,0:T(8,128)(2,1)}) custom-call(bf16[384,768]{1,0:T(8,128)(2,1)} %refs_0_.2, bf16[384,768]{1,0:T(8,128)(2,1)} %refs_1_.1, bf16[384,768]{1,0:T(8,128)(2,1)} %refs_2_.1), custom_call_target="tpu_custom_call" | custom-call | tf_op jit(solution)/shard_map/gather_0/pallas_call | solution.py:387
  75.8 0.7 pad_add_fusion.meta_ref
  76.4 0.0 copy-done.3
  76.5 0.0 all-gather.3.cloned.1.call-done
  76.5 0.0 copy-start.1
  76.5 2.5 convert_reduce_fusion
  79.1 0.3 copy-done.1
  79.4 1.0 fusion.2
  80.3 2.8 %fusion.5.refs_0_ = bf16[512,3072]{1,0:T(8,128)(2,1)S(1)} fusion(bf16[512,3072]{1,0:T(8,128)(2,1)S(1)} %copy-done.1, f32[3072]{0:T(1024)S(1)} %bitcast.21, f32[3072]{0:T(1024)S(1)} %bitcast.22, f32[3072]{0:T(1024)S(1)} %bitcast.20, f32[3072]{0:T(1024)S(1)} %bitcast.19, f32[512]{0:T(512)S(1)} %add_rsqrt_fusion, f32[512]{0:T(512)S(1)} %broadcast_multiply_fusion, ...), kind=kLoop, calls=%fused_computation.7 | loop fusion | flops 14155776 | bytes 6345216 | tf_op jit(solution)/shard_map/convert_element_type | solution.py:27
  83.1 64.2 %project_and_gather.1 = (bf16[4096,768]{1,0:T(8,128)(2,1)}, bf16[4096,768]{1,0:T(8,128)(2,1)}, bf16[512,768]{1,0:T(8,128)(2,1)S(1)}) custom-call(bf16[512,3072]{1,0:T(8,128)(2,1)S(1)} %fusion.5.refs_0_, bf16[3072,768]{1,0:T(8,128)(2,1)} %get-tuple-element.13.refs_1_, bf16[3072,768]{1,0:T(8,128)(2,1)} %get-tuple-element.14.refs_2_, ...), custom_call_target="tpu_custom_call" | custom-call | tf_op jit(solution)/shard_map/project_and_gather/pallas_call | solution.py:365
  147.3 0.0 copy-start
  147.3 0.9 copy-done
  148.2 22.3 %attend_0.1 = bf16[256,768]{1,0:T(8,128)(2,1)} custom-call(s32[2]{0:T(128)} %pad_add_fusion.meta_ref, bf16[512,768]{1,0:T(8,128)(2,1)} %copy-done, bf16[4096,768]{1,0:T(8,128)(2,1)} %get-tuple-element.17.k_ref, bf16[4096,768]{1,0:T(8,128)(2,1)} %get-tuple-element.18.v_ref), custom_call_target="tpu_custom_call" | custom-call | flops 3221225472 | bytes 12582912 | tf_op jit(solution)/shard_map/attend_0/pallas_call | solution.py:478
  170.4 0.0 all-gather.5.cloned.1.call-update
  170.5 0.1 dynamic-slice_reduce_fusion.1
  170.6 0.6 pad_add_fusion.1.meta_ref
  171.2 22.3 %attend_1.1.refs_1_ = bf16[256,768]{1,0:T(8,128)(2,1)} custom-call(s32[2]{0:T(128)} %pad_add_fusion.1.meta_ref, bf16[512,768]{1,0:T(8,128)(2,1)} %copy-done, bf16[4096,768]{1,0:T(8,128)(2,1)} %get-tuple-element.17.k_ref, bf16[4096,768]{1,0:T(8,128)(2,1)} %get-tuple-element.18.v_ref), custom_call_target="tpu_custom_call" | custom-call | flops 3221225472 | bytes 12582912 | tf_op jit(solution)/shard_map/attend_1/pallas_call | solution.py:478
  193.4 47.7 %gather_2.1 = (bf16[3072,768]{1,0:T(8,128)(2,1)}, bf16[256,3072]{1,0:T(8,128)(2,1)}) custom-call(bf16[384,768]{1,0:T(8,128)(2,1)} %refs_0_.3, bf16[256,768]{1,0:T(8,128)(2,1)} %attend_1.1.refs_1_), custom_call_target="tpu_custom_call" | custom-call | tf_op jit(solution)/shard_map/gather_2/pallas_call | solution.py:387
  241.2 4.2 %fusion.14 = f32[256,768]{1,0:T(8,128)S(1)} fusion(bf16[256,3072]{1,0:T(8,128)(2,1)} %get-tuple-element.20, bf16[3072,768]{1,0:T(8,128)(2,1)} %get-tuple-element.19), kind=kOutput, calls=%fused_computation.34 | convolution fusion | flops 1207959552 | bytes 7077888 | tf_op jit(solution)/shard_map/dot_general | solution.py:544
  245.4 0.0 copy-start.2
  245.4 0.0 all-gather.5.cloned.1.call-done
  245.4 4.3 %fusion.13 = f32[256,768]{1,0:T(8,128)S(1)} fusion(bf16[256,3072]{1,0:T(8,128)(2,1)} %all-gather.5.cloned.1.call-done, bf16[3072,768]{1,0:T(8,128)(2,1)} %get-tuple-element.19), kind=kOutput, calls=%fused_computation.33 | convolution fusion | flops 1207959552 | bytes 7077888 | tf_op jit(solution)/shard_map/dot_general | solution.py:544
  249.7 0.0 copy-done.2
  249.7 1.2 fusion.7
  (10 shorter events, 0.1 us)
Async XLA Ops:
  6.5 69.9 %copy-start.3 = (f32[6,3072]{1,0:T(8,128)S(1)}, f32[6,3072]{1,0:T(8,128)}, u32[]{:S(2)}) copy-start(f32[6,3072]{1,0:T(8,128)} %param.13) | copy-start | bytes 221188
  6.5 70.0 %all-gather.3.cloned.1.call-start = ((), (), s32[]{:S(2)}) async-start(), calls=%async_computation | async-start | bytes 3932160 | tf_op jit(solution)/shard_map/all_gather | solution.py:512
  7.3 238.2 %all-gather.5.cloned.1.call-start = ((), (), s32[]{:S(2)}) async-start(), calls=%async_computation.1 | async-start | bytes 1966080 | tf_op jit(solution)/shard_map/all_gather | solution.py:539
  76.5 2.8 %copy-start.1 = (bf16[512,3072]{1,0:T(8,128)(2,1)S(1)}, bf16[512,3072]{1,0:T(8,128)(2,1)}, u32[]{:S(2)}) copy-start(bf16[512,3072]{1,0:T(8,128)(2,1)} %all-gather.3.cloned.1.call-done) | copy-start | bytes 9437188
  147.3 0.9 copy-start
  245.4 4.3 %copy-start.2 = (bf16[512,768]{1,0:T(8,128)(2,1)S(1)}, bf16[512,768]{1,0:T(8,128)(2,1)}, u32[]{:S(2)}) copy-start(bf16[512,768]{1,0:T(8,128)(2,1)} %param.10) | copy-start | bytes 2359300
Sparse Core Ops, SparseCore 0:
  8.9 66.1 all-gather.2
  170.6 38.1 all-gather.4

commit v3 on v2

--- a/solution.py
+++ b/solution.py
@@ -476,7 +476,7 @@
     out_block = pl.BlockSpec((own_rows, lanes), lambda pair, meta: (0, pair))
     full = pl.BlockSpec((count, lanes), lambda pair, meta: (0, pair))
     return pl.pallas_call(
-        functools.partial(attend_kernel, 256, 512, head_width),
+        functools.partial(attend_kernel, min(256, own_rows), 512, head_width),
         out_shape=jax.ShapeDtypeStruct((own_rows, width), jnp.bfloat16),
         grid_spec=pltpu.PrefetchScalarGridSpec(
             num_scalar_prefetch=1,
@@ -490,7 +490,7 @@
             bytes_accessed=4 * count * width,
             transcendentals=own_rows * count * width // head_width,
         ),
-        name=f"attend_{part}",
+        name=f"attend_{part}_{parts}",
     )(meta, query, keys, values)
 
 
@@ -532,11 +532,13 @@
         1,
     )
     first_row = lax.axis_index("tok") * own_rows
-    first, second = (
-        attend(query_flat, keys, values, bound, first_row, head_width, part, 2)
-        for part in range(2)
-    )
-    first_heads = lax.all_gather(first, "mdl", axis=1, tiled=True)
+    early, middle, second = (
+        attend(query_flat, keys, values, bound, first_row, head_width, part, parts)
+        for part, parts in ((0, 4), (1, 4), (1, 2))
+    )
+    first_heads = jnp.concatenate(
+        [lax.all_gather(piece, "mdl", axis=1, tiled=True) for piece in (early, middle)], axis=0
+    )
     out_full, second_heads = gather_all(mesh, [out_weight], [second], 2)
     out_width = out_weight.shape[1]
     projected = jnp.concatenate(

time: 257 us -> 303 us (1.18)
  blocking collectives: 0 us -> 38.6 us
  Pallas kernels: 221 us -> 233 us
    all_gather x0 -> x2, blocking collectives: none -> 38.6 us  [shards(): lax.all_gather(piece, 'mdl', axis=1, tiled=True)]
    pallas_call x2 -> x3, Pallas kernels: 44.5 us -> 60.8 us  [attend(): pl.pallas_call(functools.partial(attend_kernel, min(256, own_rows), 512,...]
    pallas_call x2, Pallas kernels: 113 us -> 108 us  [gather_all(): pl.pallas_call(functools.partial(gather_kernel, n_tok, n_mdl, n_row, n_co...]
  transfers between devices with their start and end apart: 2 -> 1, of which waited for: 0 -> 0; matrix products, arithmetic and copies ran while one was open for 3% -> 2% of each run, Pallas kernels for 52% -> 21%
where the time goes in v3:
time: 303 us; the launch traced here: 306 us
  Pallas kernels  233 us (77%)
  blocking collectives  38.6 us (13%)
  between operations  14.3 us (5%)
  other arithmetic  10.2 us (3%)
  matrix products  5.77 us (2%)
  local copies, waits for them, and re-layouts  3.1 us (1%)
    pallas_call x2, Pallas kernels, gather_all(): pl.pallas_call(functools.partial(gather_kernel, n_tok, n_mdl, n_row, n_co...  108 us
    pallas_call x1, Pallas kernels, project_and_gather(): pl.pallas_call(functools.partial(project_kernel, n_tok, n_mdl, head_width...  64.2 us
    pallas_call x3, Pallas kernels, attend(): pl.pallas_call(functools.partial(attend_kernel, min(256, own_rows), 512,...  60.8 us
    all_gather x2, blocking collectives, shards(): lax.all_gather(piece, 'mdl', axis=1, tiled=True)  38.6 us
  transfers between devices with their start and end apart: 1, of which 0 were waited for; matrix products, arithmetic and copies ran while one was open for 2% of the time, Pallas kernels for 21%

profile of v3, /device:TPU:0, one launch (start us, length us, event | category | flops | bytes accessed | tf_op | source)
XLA Modules:
  0.0 306.0 jit_solution(9974551815651525978)
XLA Ops:
  6.5 0.0 copy-start.3
  6.5 0.0 all-gather.2.cloned.1.call-start
  6.5 0.7 all-gather.2.cloned.1.call-update
  7.3 0.7 convert_element_type.33
  8.7 0.3 fusion.15
  9.1 0.1 copy.12.refs_7_
  9.2 0.1 copy.11.refs_6_
  9.4 0.7 tile.12
  10.0 0.1 broadcast_in_dim_tile.6.refs_4_
  10.1 0.7 tile.13
  10.8 0.1 broadcast_in_dim_tile.7.refs_5_
  10.8 64.9 %gather_0.1 = (bf16[3072,768]{1,0:T(8,128)(2,1)}, bf16[3072,768]{1,0:T(8,128)(2,1)}, bf16[3072,768]{1,0:T(8,128)(2,1)}) custom-call(bf16[384,768]{1,0:T(8,128)(2,1)} %refs_0_.2, bf16[384,768]{1,0:T(8,128)(2,1)} %refs_1_.1, bf16[384,768]{1,0:T(8,128)(2,1)} %refs_2_.1), custom_call_target="tpu_custom_call" | custom-call | tf_op jit(solution)/shard_map/gather_0/pallas_call | solution.py:387
  75.7 0.0 copy-done.3
  75.7 0.1 dynamic-slice_reduce_fusion.1
  75.8 0.6 pad_add_fusion.meta_ref
  76.5 0.7 pad_add_fusion.1.meta_ref
  77.1 0.6 pad_add_fusion.2.meta_ref
  77.8 0.0 all-gather.2.cloned.1.call-done
  77.8 0.0 copy-start.1
  77.8 2.5 convert_reduce_fusion
  80.3 0.3 copy-done.1
  80.6 1.0 fusion.2
  81.6 2.6 fusion.5.refs_0_
  84.2 64.2 %project_and_gather.1 = (bf16[4096,768]{1,0:T(8,128)(2,1)}, bf16[4096,768]{1,0:T(8,128)(2,1)}, bf16[512,768]{1,0:T(8,128)(2,1)S(1)}) custom-call(bf16[512,3072]{1,0:T(8,128)(2,1)S(1)} %fusion.5.refs_0_, bf16[3072,768]{1,0:T(8,128)(2,1)} %get-tuple-element.13.refs_1_, bf16[3072,768]{1,0:T(8,128)(2,1)} %get-tuple-element.14.refs_2_, ...), custom_call_target="tpu_custom_call" | custom-call | tf_op jit(solution)/shard_map/project_and_gather/pallas_call | solution.py:365
  148.4 0.0 copy-start
  148.4 0.9 copy-done
  149.3 19.2 %attend_0_4.1 = bf16[128,768]{1,0:T(8,128)(2,1)} custom-call(s32[2]{0:T(128)} %pad_add_fusion.meta_ref, bf16[512,768]{1,0:T(8,128)(2,1)} %copy-done, bf16[4096,768]{1,0:T(8,128)(2,1)} %get-tuple-element.17.k_ref, bf16[4096,768]{1,0:T(8,128)(2,1)} %get-tuple-element.18.v_ref), custom_call_target="tpu_custom_call" | custom-call | flops 1610612736 | bytes 12582912 | tf_op jit(solution)/shard_map/attend_0_4/pallas_call | solution.py:478
  168.5 20.0 %all_gather.10 = bf16[128,3072]{1,0:T(8,128)(2,1)S(1)} all-gather(bf16[128,768]{1,0:T(8,128)(2,1)} %attend_0_4.1), channel_id=1, replica_groups=mesh['tok'=8,'mdl'=4] {'mdl'}, dimensions={1}, use_global_device_ids=true | all-gather | bytes 983040 | tf_op jit(solution)/shard_map/all_gather | solution.py:540
  188.5 19.3 %attend_1_4.1 = bf16[128,768]{1,0:T(8,128)(2,1)} custom-call(s32[2]{0:T(128)} %pad_add_fusion.1.meta_ref, bf16[512,768]{1,0:T(8,128)(2,1)} %copy-done, bf16[4096,768]{1,0:T(8,128)(2,1)} %get-tuple-element.17.k_ref, bf16[4096,768]{1,0:T(8,128)(2,1)} %get-tuple-element.18.v_ref), custom_call_target="tpu_custom_call" | custom-call | flops 1610612736 | bytes 12582912 | tf_op jit(solution)/shard_map/attend_1_4/pallas_call | solution.py:478
  207.8 18.6 %all_gather.11 = bf16[128,3072]{1,0:T(8,128)(2,1)S(1)} all-gather(bf16[128,768]{1,0:T(8,128)(2,1)} %attend_1_4.1), channel_id=1, replica_groups=mesh['tok'=8,'mdl'=4] {'mdl'}, dimensions={1}, use_global_device_ids=true | all-gather | bytes 983040 | tf_op jit(solution)/shard_map/all_gather | solution.py:540
  226.4 22.3 %attend_1_2.1.refs_1_ = bf16[256,768]{1,0:T(8,128)(2,1)} custom-call(s32[2]{0:T(128)} %pad_add_fusion.2.meta_ref, bf16[512,768]{1,0:T(8,128)(2,1)} %copy-done, bf16[4096,768]{1,0:T(8,128)(2,1)} %get-tuple-element.17.k_ref, bf16[4096,768]{1,0:T(8,128)(2,1)} %get-tuple-element.18.v_ref), custom_call_target="tpu_custom_call" | custom-call | flops 3221225472 | bytes 12582912 | tf_op jit(solution)/shard_map/attend_1_2/pallas_call | solution.py:478
  248.6 43.4 %gather_2.1 = (bf16[3072,768]{1,0:T(8,128)(2,1)}, bf16[256,3072]{1,0:T(8,128)(2,1)}) custom-call(bf16[384,768]{1,0:T(8,128)(2,1)} %refs_0_.3, bf16[256,768]{1,0:T(8,128)(2,1)} %attend_1_2.1.refs_1_), custom_call_target="tpu_custom_call" | custom-call | tf_op jit(solution)/shard_map/gather_2/pallas_call | solution.py:387
  292.1 0.0 slice-start
  292.1 0.0 slice-start.1
  292.1 4.3 %fusion.18 = f32[256,768]{1,0:T(8,128)S(1)} fusion(bf16[256,3072]{1,0:T(8,128)(2,1)} %get-tuple-element.20, bf16[3072,768]{1,0:T(8,128)(2,1)} %get-tuple-element.19), kind=kOutput, calls=%fused_computation.39 | convolution fusion | flops 1207959552 | bytes 7077888 | tf_op jit(solution)/shard_map/dot_general | solution.py:546
  296.4 0.0 slice-done
  296.4 0.0 slice-done.1
  296.4 0.0 copy-start.2
  296.5 1.4 fusion.6
  297.9 0.0 copy-done.2
  297.9 1.2 fusion.11
  (11 shorter events, 0.1 us)
Async XLA Ops:
  6.5 69.2 %copy-start.3 = (f32[6,3072]{1,0:T(8,128)S(1)}, f32[6,3072]{1,0:T(8,128)}, u32[]{:S(2)}) copy-start(f32[6,3072]{1,0:T(8,128)} %param.13) | copy-start | bytes 221188
  6.5 71.2 %all-gather.2.cloned.1.call-start = ((), (), s32[]{:S(2)}) async-start(), calls=%async_computation | async-start | bytes 3932160 | tf_op jit(solution)/shard_map/all_gather | solution.py:512
  77.8 2.8 copy-start.1
  148.4 0.9 copy-start
  292.1 4.4 %slice-start = ((s8[4718592]{0:T(1024)(128)(4,1)}), s8[4194304]{0:T(1024)(128)(4,1)S(1)}, s32[]{:S(2)}) async-start(s8[4718592]{0:T(1024)(128)(4,1)} %bitcast.26), calls=%async_computation.1 | async-start | bytes 8388608
  292.1 4.4 %slice-start.1 = ((s8[4718592]{0:T(1024)(128)(4,1)}), s8[524288]{0:T(1024)(128)(4,1)S(1)}, s32[]{:S(2)}) async-start(s8[4718592]{0:T(1024)(128)(4,1)} %bitcast.26), calls=%async_computation.2 | async-start | bytes 1048576
  296.4 1.5 copy-start.2
Sparse Core Ops, SparseCore 0:
  8.9 66.1 all-gather.1
